TPU v7x, 256 devices: a whole 4x4x8 slice. The times are simulated.
256 devices in a mesh: group: 32 (over y, z), pencil: 8 (over x, core).
Axes of the slice: x: 4, y: 4, z: 8, core: 2. Of those that a mesh axis runs over, the one named last changes fastest.
Arguments:
- mult_iterate: float32 [32, 8, 8192], P('group', 'pencil'), may hold values from -6 to 6
- residual: float32 [32, 8, 8192], P('group', 'pencil'), may hold values from -6 to 6
- direction: float32 [32, 8, 8192], P('group', 'pencil'), may hold values from -6 to 6
- mult_scale: float32 [32, 8, 8192], P('group', 'pencil'), may hold values from 0.5 to 18
- eigen_basis: float32 [128, 3, 64, 64], P('group'), may hold values from -1 to 1
- eigen_values: float32 [128, 3, 64], P('group'), may hold values from 0.2 to 2
- elastic_coef: float32 [128, 3, 3], P('group'), may hold values from 0.5 to 2
- coarse_inverse: float32 [1024, 1024], replicated, may hold values from -1 to 2.5
- send_pos: int32 [32, 8, 16384], P('group', 'pencil'), may hold values from 0 to 24191, as said below
- pair_slots: int32 [32, 8, 2, 8192], P('group', 'pencil'), may hold values from 0 to 16383, as said below
- prim_rows: int32 [32, 8, 32], P('group', 'pencil'), may hold values from 0 to 16383, as said below
- coarse_idx: int32 [32, 8, 32], P('group', 'pencil'), may hold values from 0 to 1023
Outputs:
- new_iterate: float32 [32, 8, 8192], P('group', 'pencil')
- new_residual: float32 [32, 8, 8192], P('group', 'pencil')
- new_direction: float32 [32, 8, 8192], P('group', 'pencil')
Inputs may be any that keep to these rules, and one draw needn't show every extreme that they name: `send_pos`: distinct within each block (g, s). `pair_slots`: in each block (g, s) the two rows together hold every number of 0 to 16383 once. `prim_rows`: distinct within each block (g, s).
All inputs are finite; a program needn't handle non-finite values.
Results may differ from a plain program's by a relative error of at most 0.0003.
Values sent between devices are 32-bit elements; how exact they have to be, the bound alone decides.
No kernel may reach another device: no remote copies, remote signals or barrier semaphores. Data moves between devices by JAX's collectives and lax.ppermute only.
A program may use at most 128 MiB of HBM per device.

v0:
```python
import jax
import jax.numpy as jnp
from jax import lax
from jax.sharding import PartitionSpec as P


def cycle_slot(index, extent):
    cycle_size = 4 * extent - 4
    plane_index = index // cycle_size
    cycle_spot = index % cycle_size
    side_slot = jnp.where(
        cycle_spot < extent,
        cycle_spot,
        jnp.where(
            cycle_spot < 2 * extent - 2,
            cycle_spot + 1,
            jnp.where(cycle_spot < 3 * extent - 4, cycle_spot + 3, cycle_spot + 4),
        ),
    )
    return plane_index * 4 * extent + side_slot


def cycle_to_volume(cycles, extent):
    sides = cycles.reshape(cycles.shape[:-1] + (4, extent))
    count = jnp.arange(extent, dtype=jnp.int32)
    first_edge = (count == 0).astype(jnp.float32)
    last_edge = (count == extent - 1).astype(jnp.float32)
    plane = sides[..., 0, None, :] * first_edge[:, None]
    plane = plane + sides[..., 1, :, None] * first_edge[None, :]
    plane = plane + sides[..., 2, :, None] * last_edge[None, :]
    return plane + sides[..., 3, None, :] * last_edge[:, None]


def volume_to_cycle(volume):
    sides = jnp.stack(
        [volume[..., 0, :], volume[..., :, 0], volume[..., :, -1], volume[..., -1, :]], axis=-2
    )
    return sides.reshape(volume.shape[:-2] + (4 * volume.shape[-1],))


def spectrum(coeffs, along_x, along_y, along_z):
    first = coeffs[None, :, :, 0, None, None] * along_x.T[:, :, None, None, None]
    second = coeffs[None, :, :, 1, None, None] * along_y[None, :, None, :, None]
    third = coeffs[None, :, :, 2, None, None] * along_z[None, :, None, None, :]
    return first + second + third


def forward_yz(volume, basis):
    highest = lax.Precision.HIGHEST
    step_one = jnp.einsum("xpcyz,pzk->xpcyk", volume, basis[:, 2], precision=highest)
    return jnp.einsum("xpcyk,pyj->xpcjk", step_one, basis[:, 1], precision=highest)


def backward_yz(volume, basis):
    highest = lax.Precision.HIGHEST
    step_one = jnp.einsum("xpcjk,pyj->xpcyk", volume, basis[:, 1], precision=highest)
    return jnp.einsum("xpcyk,pzk->xpcyz", step_one, basis[:, 2], precision=highest)


def load_slab(arrived_rows, positions, slab_shape):
    cycle_total = slab_shape[0] * slab_shape[1] * slab_shape[2] * 4 * slab_shape[3]
    cycles = jnp.zeros((cycle_total,), jnp.float32).at[positions].set(arrived_rows)
    cycles = cycles.reshape(slab_shape[0], slab_shape[1], slab_shape[2], 4 * slab_shape[3])
    return cycle_to_volume(cycles, slab_shape[3])


def apply_inverse(arrived_rows, cycle_cells, basis, values, coeffs):
    highest = lax.Precision.HIGHEST
    pencils = lax.axis_size("pencil")
    extent = basis.shape[-1]
    patches = basis.shape[0]
    components = coeffs.shape[1]
    slab_x = extent // pencils
    slab_shape = (slab_x, patches, components, extent, extent)
    my_slab = lax.axis_index("pencil")
    row_start = my_slab * slab_x
    positions = cycle_slot(cycle_cells, extent)
    partial_yz = forward_yz(load_slab(arrived_rows, positions, slab_shape), basis)
    columns = lax.all_to_all(
        partial_yz.reshape(slab_x, patches, components, extent * extent),
        "pencil",
        split_axis=3,
        concat_axis=0,
        tiled=True,
    )
    columns = columns.reshape(extent, patches, components, slab_x, extent)
    spectral = jnp.einsum("xpcjk,pxi->ipcjk", columns, basis[:, 0], precision=highest)
    along_y = lax.dynamic_slice_in_dim(values[:, 1], row_start, slab_x, 1)
    scaled = spectral / spectrum(coeffs, values[:, 0], along_y, values[:, 2])
    mixed = jnp.einsum("ipcjk,pxi->xpcjk", scaled, basis[:, 0], precision=highest)
    mixed = mixed.reshape(extent, patches, components, slab_x * extent)
    back_x = lax.all_to_all(mixed, "pencil", split_axis=0, concat_axis=3, tiled=True).reshape(
        slab_shape
    )
    displace = backward_yz(back_x, basis)
    return volume_to_cycle(displace).reshape(-1)[positions]


def body(
    mult_iterate,
    residual,
    direction,
    mult_scale,
    eigen_basis,
    eigen_values,
    elastic_coef,
    coarse_inverse,
    send_pos,
    pair_slots,
    prim_rows,
    coarse_idx,
):
    highest = lax.Precision.HIGHEST
    groups = lax.axis_size("group")
    iterate_now = mult_iterate[0, 0]
    resid_now = residual[0, 0]
    search_dir = direction[0, 0]
    scale_now = mult_scale[0, 0]
    pair_rows = pair_slots[0, 0]
    cycle_cells = send_pos[0, 0]
    primal = prim_rows[0, 0]
    coarse_ids = coarse_idx[0, 0]
    rows_count = cycle_cells.shape[0]
    per_owner = rows_count // groups
    coarse_count = coarse_inverse.shape[0]
    old_part = jnp.sum(resid_now * scale_now * resid_now)
    old_norm = lax.psum(old_part, ("group", "pencil"))
    back_rows = (
        jnp.zeros((rows_count,), jnp.float32)
        .at[pair_rows[0]]
        .set(search_dir)
        .at[pair_rows[1]]
        .set(-search_dir)
    )
    arrived_rows = lax.all_to_all(
        back_rows.reshape(groups, per_owner), "group", split_axis=0, concat_axis=0, tiled=True
    ).reshape(rows_count)
    picked = apply_inverse(arrived_rows, cycle_cells, eigen_basis, eigen_values, elastic_coef)
    onehot = (coarse_ids[:, None] == jnp.arange(coarse_count, dtype=jnp.int32)[None, :]).astype(
        jnp.float32
    )
    local_coarse = jnp.dot(picked[primal], onehot, precision=highest)
    total_coarse = lax.psum(local_coarse, ("group", "pencil"))
    lifted = jnp.dot(coarse_inverse, total_coarse, precision=highest)
    sent_rows = picked.at[primal].add(jnp.dot(onehot, lifted, precision=highest))
    owner_rows = lax.all_to_all(
        sent_rows.reshape(groups, per_owner), "group", split_axis=0, concat_axis=0, tiled=True
    ).reshape(rows_count)
    mapped = owner_rows[pair_rows[0]] - owner_rows[pair_rows[1]]
    curvature = lax.psum(jnp.sum(search_dir * mapped), ("group", "pencil"))
    step_size = old_norm / curvature
    iterate_next = iterate_now + step_size * search_dir
    resid_next = resid_now - step_size * mapped
    precond = scale_now * resid_next
    norm_next = lax.psum(jnp.sum(resid_next * precond), ("group", "pencil"))
    search_next = precond + norm_next / old_norm * search_dir
    return (iterate_next[None, None], resid_next[None, None], search_next[None, None])


def solution(mesh):
    in_specs = (
        P("group", "pencil", None),
        P("group", "pencil", None),
        P("group", "pencil", None),
        P("group", "pencil", None),
        P("group", None, None, None),
        P("group", None, None),
        P("group", None, None),
        P(),
        P("group", "pencil", None),
        P("group", "pencil", None, None),
        P("group", "pencil", None),
        P("group", "pencil", None),
    )
    out_specs = (P("group", "pencil", None), P("group", "pencil", None), P("group", "pencil", None))
    return jax.shard_map(body, mesh=mesh, in_specs=in_specs, out_specs=out_specs, check_vma=False)
```

profile of v0, /device:TPU:1, one launch (start us, length us, event | category | flops | bytes accessed | tf_op | source)
XLA Modules:
  0.0 876.2 jit_solution(14388846261782737221)
XLA Ops:
  2.4 31.2 %scatter_custom_fusion = f32[16384]{0:T(1024)} fusion(s32[8192]{0:T(1024)S(1)} %bitcast.164, f32[8192]{0:T(1024)} %bitcast.154, f32[]{:T(128)} %constant.16.clone.1), kind=kCustom, calls=%fused_computation.81 | custom fusion | bytes 66048 | tf_op jit(solution)/shard_map/scatter | solution.py:131
  33.7 31.9 %scatter_fusion = f32[16384]{0:T(1024)} fusion(f32[16384]{0:T(1024)} %scatter_custom_fusion, s32[8192]{0:T(1024)S(1)} %bitcast.151, f32[8192]{0:T(1024)S(1)} %neg.3), kind=kCustom, calls=%fused_computation.5 | custom fusion | bytes 131072 | tf_op jit(solution)/shard_map/scatter | solution.py:133
  65.6 12.0 %all-to-all-start = ((f32[32,1,512]{2,1,0:T(1,128)}), f32[32,1,512]{2,1,0:T(1,128)S(1)}, u32[]{:S(2)}, u32[]{:S(2)}) async-start(f32[32,1,512]{2,1,0:T(1,128)} %bitcast.11), calls=%async_computation | async-start | bytes 131072 | tf_op jit(solution)/shard_map/all_to_all | solution.py:135
  78.5 8.0 all-to-all-done
  86.5 60.8 %scatter_custom_fusion.2 = f32[24576]{0:T(1024)S(1)} fusion(s32[16384]{0:T(1024)S(1)} %bitcast.160, f32[16384]{0:T(1024)S(1)} %bitcast.167, f32[]{:T(128)} %constant.16.clone.1), kind=kCustom, calls=%fused_computation.72 | custom fusion | bytes 98308 | tf_op jit(solution)/shard_map/scatter | solution.py:62
  147.7 4.0 fusion.8
  151.7 5.2 fusion.16
  156.9 34.6 %copy.135 = f32[8,4,3,64,64]{0,1,2,4,3:T(4,128)} copy(f32[8,4,3,64,64]{3,4,2,0,1:T(8,128)S(1)} %fusion.16) | data formatting | bytes 3145728 | tf_op jit(solution)/shard_map/reshape | solution.py:80
  191.5 31.9 %reshape.387 = f32[8,1,49152]{2,1,0:T(1,128)} reshape(f32[4096,3,4,8]{3,2,1,0:T(4,128)} %bitcast.146) | data formatting | bytes 3145728
  223.4 6.5 all-to-all-start.1
  231.3 19.2 %all-to-all-done.1 = f32[8,1,49152]{2,1,0:T(1,128)S(1)} async-done(((f32[8,1,49152]{2,1,0:T(1,128)}), f32[8,1,49152]{2,1,0:T(1,128)S(1)}, u32[]{:S(2)}, u32[]{:S(2)}) %all-to-all-start.1) | async-done | bytes 1572896 | tf_op jit(solution)/shard_map/all_to_all | solution.py:79
  251.0 4.4 reduce
  255.4 38.7 %reshape.388 = f32[4096,3,4,8]{3,2,1,0:T(4,128)} reshape(f32[8,49152]{1,0:T(8,128)S(1)} %reduce) | data formatting | bytes 3145728
  294.1 20.7 %copy.137 = f32[8,4,3,8,512]{4,0,3,2,1:T(8,128)} copy(f32[8,4,3,8,512]{0,1,2,4,3:T(4,128)} %bitcast.147) | data formatting | bytes 3145728 | tf_op jit(solution)/shard_map/all_to_all | solution.py:79
  314.8 2.6 reshape.305
  317.4 5.1 fusion.5
  322.5 3.2 fusion.2
  327.8 4.6 all-to-all-start.2
  333.7 19.3 %all-to-all-done.2 = f32[64,4,3,512]{3,1,2,0:T(4,128)S(1)} async-done(((f32[64,4,3,512]{3,1,2,0:T(4,128)}), f32[64,4,3,512]{3,1,2,0:T(4,128)S(1)}, u32[]{:S(2)}, u32[]{:S(2)}) %all-to-all-start.2) | async-done | bytes 1572896 | tf_op jit(solution)/shard_map/all_to_all | solution.py:92
  355.6 2.6 reshape.382
  358.3 5.1 fusion.35
  363.4 5.1 fusion.19
  368.5 2.7 fusion.58
  375.9 160.4 %gather_fusion = f32[16384]{0:T(1024)} fusion(f32[24576]{0:T(1024)S(1)} %reshape_reshape.7, s32[16384]{0:T(1024)S(1)} %copy-done.8), kind=kCustom, calls=%fused_computation | custom fusion | bytes 196608 | tf_op jit(solution)/shard_map/gather | solution.py:96
  538.1 72.8 %psum.29 = f32[1024]{0:T(1024)S(1)} all-reduce(f32[1024]{0:T(1024)S(1)} %bitcast.172), channel_id=1, replica_groups=mesh['group'=32,'pencil'=8] {'group','pencil'}, use_global_device_ids=true, to_apply=%region_5.6 | all-reduce | flops 1024 | bytes 8192 | tf_op jit(solution)/shard_map/psum | solution.py:143
  610.9 5.6 convolution_bitcast_fusion
  619.0 5.0 all-to-all-start.3
  624.7 8.2 all-to-all-done.3
  632.9 45.5 %gather_fusion.3 = f32[8192]{0:T(1024)S(1)} fusion(f32[16384]{0:T(1024)S(1)} %bitcast.144, s32[8192]{0:T(1024)S(1)} %copy-done.11), kind=kCustom, calls=%fused_computation.3 | custom fusion | bytes 98304 | tf_op jit(solution)/shard_map/gather | solution.py:149
  678.5 45.5 %gather_fusion.2 = f32[8192]{0:T(1024)S(1)} fusion(f32[16384]{0:T(1024)S(1)} %bitcast.145, s32[8192]{0:T(1024)S(1)} %broadcast_clamp_fusion.2), kind=kCustom, calls=%fused_computation.2 | custom fusion | bytes 98304 | tf_op jit(solution)/shard_map/gather | solution.py:149
  724.6 73.3 %all-reduce = (f32[]{:T(128)}, f32[]{:T(128)}) all-reduce(f32[]{:T(128)} %fusion.51, f32[]{:T(128)} %get-tuple-element.9), channel_id=1, replica_groups=mesh['group'=32,'pencil'=8] {'group','pencil'}, use_global_device_ids=true, to_apply=%region_1.0 | all-reduce | flops 2 | bytes 16 | tf_op jit(solution)/shard_map/psum | solution.py:127
  799.9 74.0 %psum.31 = f32[]{:T(128)} all-reduce(f32[]{:T(128)} %get-tuple-element.7), channel_id=1, replica_groups=mesh['group'=32,'pencil'=8] {'group','pencil'}, use_global_device_ids=true, to_apply=%region_10.11 | all-reduce | flops 1 | bytes 8 | tf_op jit(solution)/shard_map/psum | solution.py:155
  (85 shorter events, 22.2 us)
Async XLA Ops:
  1.6 64.0 %copy-start.1 = (s32[8192,1]{0,1:T(1,128)}, s32[8192,1]{0,1:T(1,128)S(1)}, u32[]{:S(2)}) copy-start(s32[8192,1]{0,1:T(1,128)S(1)} %get-tuple-element.19) | copy-start | bytes 98308
  1.6 63.9 %copy-start.9 = (s32[8192,1]{0,1:T(1,128)}, s32[8192,1]{0,1:T(1,128)S(1)}, u32[]{:S(2)}) copy-start(s32[8192,1]{0,1:T(1,128)S(1)} %get-tuple-element.20) | copy-start | bytes 98308
  33.7 44.0 %copy-start.12 = (s32[1,1,16384]{2,1,0:T(1,128)S(1)}, s32[1,1,16384]{2,1,0:T(1,128)}, u32[]{:S(2)}) copy-start(s32[1,1,16384]{2,1,0:T(1,128)} %param.20) | copy-start | bytes 196612
  33.7 114.0 %copy-start = (f32[4,3,64,64]{3,2,1,0:T(8,128)S(1)}, f32[4,3,64,64]{3,2,1,0:T(8,128)}, u32[]{:S(2)}) copy-start(f32[4,3,64,64]{3,2,1,0:T(8,128)} %param.16) | copy-start | bytes 589828
  65.6 20.9 %all-to-all-start = ((f32[32,1,512]{2,1,0:T(1,128)}), f32[32,1,512]{2,1,0:T(1,128)S(1)}, u32[]{:S(2)}, u32[]{:S(2)}) async-start(f32[32,1,512]{2,1,0:T(1,128)} %bitcast.11), calls=%async_computation | async-start | bytes 131072 | tf_op jit(solution)/shard_map/all_to_all | solution.py:135
  78.4 8.1 copy-start.6
  223.4 6.5 copy-start.13
  223.4 7.0 copy-start.16
  223.4 27.1 %all-to-all-start.1 = ((f32[8,1,49152]{2,1,0:T(1,128)}), f32[8,1,49152]{2,1,0:T(1,128)S(1)}, u32[]{:S(2)}, u32[]{:S(2)}) async-start(f32[8,1,49152]{2,1,0:T(1,128)} %reshape.387), calls=%async_computation.1 | async-start | bytes 3145728 | tf_op jit(solution)/shard_map/all_to_all | solution.py:79
  317.4 5.1 copy-start.14
  325.8 6.7 copy-start.17
  327.8 4.6 copy-start.2
  327.8 5.2 copy-start.7
  327.8 25.2 %all-to-all-start.2 = ((f32[64,4,3,512]{3,1,2,0:T(4,128)}), f32[64,4,3,512]{3,1,2,0:T(4,128)S(1)}, u32[]{:S(2)}, u32[]{:S(2)}) async-start(f32[64,4,3,512]{3,1,2,0:T(4,128)} %copy.119), calls=%async_computation.2 | async-start | bytes 3145728 | tf_op jit(solution)/shard_map/all_to_all | solution.py:92
  371.3 4.6 copy-start.8
  375.9 162.0 %copy-start.18 = (s32[1,1,32]{2,1,0:T(1,128)S(1)}, s32[1,1,32]{2,1,0:T(1,128)}, u32[]{:S(2)}) copy-start(s32[1,1,32]{2,1,0:T(1,128)} %param.23) | copy-start | bytes 388
  536.3 87.7 %copy-start.10 = (s32[8192,1]{0,1:T(1,128)S(1)}, s32[8192,1]{0,1:T(1,128)}, u32[]{:S(2)}) copy-start(s32[8192,1]{0,1:T(1,128)} %copy-done.9) | copy-start | bytes 98308
  536.3 87.7 %copy-start.4 = (f32[1,1,8192]{2,1,0:T(1,128)S(1)}, f32[1,1,8192]{2,1,0:T(1,128)}, u32[]{:S(2)}) copy-start(f32[1,1,8192]{2,1,0:T(1,128)} %param.15) | copy-start | bytes 98308
  536.3 87.7 %copy-start.5 = (f32[1,1,8192]{2,1,0:T(1,128)S(1)}, f32[1,1,8192]{2,1,0:T(1,128)}, u32[]{:S(2)}) copy-start(f32[1,1,8192]{2,1,0:T(1,128)} %param.13) | copy-start | bytes 98308
  536.3 96.6 %copy-start.11 = (s32[8192]{0:T(1024)S(1)}, s32[8192]{0:T(1024)}, u32[]{:S(2)}) copy-start(s32[8192]{0:T(1024)} %broadcast_clamp_fusion.1) | copy-start | bytes 98308
  619.0 13.9 %all-to-all-start.3 = ((f32[32,1,512]{2,1,0:T(1,128)}), f32[32,1,512]{2,1,0:T(1,128)S(1)}, u32[]{:S(2)}, u32[]{:S(2)}) async-start(f32[32,1,512]{2,1,0:T(1,128)} %bitcast.57), calls=%async_computation.3 | async-start | bytes 131072 | tf_op jit(solution)/shard_map/all_to_all | solution.py:146
  678.4 45.6 %copy-start.3 = (f32[1,1,8192]{2,1,0:T(1,128)S(1)}, f32[1,1,8192]{2,1,0:T(1,128)}, u32[]{:S(2)}) copy-start(f32[1,1,8192]{2,1,0:T(1,128)} %param.14) | copy-start | bytes 98308
  678.4 196.8 %copy-start.15 = (f32[1,1,8192]{2,1,0:T(1,128)S(1)}, f32[1,1,8192]{2,1,0:T(1,128)}, u32[]{:S(2)}) copy-start(f32[1,1,8192]{2,1,0:T(1,128)} %param.12) | copy-start | bytes 98308
where the time goes:
time: 881 us; the launch traced here: 876 us
  local copies, waits for them, and re-layouts  521 us (59%)
  blocking collectives  220 us (25%)
  waiting for transfers between devices  54.7 us (6%)
  matrix products  33.9 us (4%)
  starting transfers between devices  28.2 us (3%)
  other arithmetic  14.1 us (2%)
    gather x1, local copies, waits for them, and re-layouts, apply_inverse(): return volume_to_cycle(displace).reshape(-1)[positions]  160 us
    gather x2, local copies, waits for them, and re-layouts, body(): mapped = owner_rows[pair_rows[0]] - owner_rows[pair_rows[1]]  91.1 us
    psum x1, blocking collectives, body(): norm_next = lax.psum(jnp.sum(resid_next * precond), ('group', 'pencil'))  74 us
    psum x1, blocking collectives, body(): old_norm = lax.psum(old_part, ('group', 'pencil'))  73.3 us
    psum x1, blocking collectives, body(): total_coarse = lax.psum(local_coarse, ('group', 'pencil'))  72.8 us
    unnamed x40, local copies, waits for them, and re-layouts  70.6 us
    scatter x2, local copies, waits for them, and re-layouts, body(): back_rows = jnp.zeros((rows_count,), jnp.float32).at[pair_rows[0]].set(se...  63.2 us
    scatter x1, local copies, waits for them, and re-layouts, load_slab(): jnp.zeros((cycle_total,), jnp.float32).at[positions].set(arrived_rows)  60.8 us
  transfers between devices with their start and end apart: 4, of which 4 were waited for; matrix products, arithmetic and copies ran while one was open for 0% of the time, Pallas kernels for 0%

commit v1 on v0

--- a/solution.py
+++ b/solution.py
@@ -140,7 +140,10 @@
         jnp.float32
     )
     local_coarse = jnp.dot(picked[primal], onehot, precision=highest)
-    total_coarse = lax.psum(local_coarse, ("group", "pencil"))
+    clear_skins = lambda incoming_x: jnp.sum(
+        lax.all_gather(incoming_x, ("group", "pencil")), axis=0
+    )
+    total_coarse = clear_skins(local_coarse)
     lifted = jnp.dot(coarse_inverse, total_coarse, precision=highest)
     sent_rows = picked.at[primal].add(jnp.dot(onehot, lifted, precision=highest))
     owner_rows = lax.all_to_all(

time: 881 us -> 924 us (1.049)
  waiting for transfers between devices: 54.7 us -> 152 us
  blocking collectives: 220 us -> 148 us
  between operations: 4 us -> 17.4 us
    all_gather x0 -> x1, waiting for transfers between devices: none -> 96.7 us  [body(): lax.all_gather(incoming_x, ('group', 'pencil'))]
    psum x1 -> x0, blocking collectives: 72.8 us -> none  [body(): total_coarse = lax.psum(local_coarse, ('group', 'pencil'))]
    unnamed x40 -> x38, local copies, waits for them, and re-layouts: 70.6 us -> 70.6 us
  transfers between devices with their start and end apart: 4 -> 5, of which waited for: 4 -> 5; matrix products, arithmetic and copies ran while one was open for 0% -> 0% of each run, Pallas kernels for 0% -> 0%
where the time goes in v1:
time: 924 us; the launch traced here: 919 us
  local copies, waits for them, and re-layouts  522 us (56%)
  waiting for transfers between devices  152 us (16%)
  blocking collectives  148 us (16%)
  matrix products  34.5 us (4%)
  starting transfers between devices  30.6 us (3%)
  between operations  17.4 us (2%)
  other arithmetic  13.6 us (1%)
    gather x1, local copies, waits for them, and re-layouts, apply_inverse(): return volume_to_cycle(displace).reshape(-1)[positions]  160 us
    all_gather x1, waiting for transfers between devices, body(): lax.all_gather(incoming_x, ('group', 'pencil'))  96.7 us
    gather x2, local copies, waits for them, and re-layouts, body(): mapped = owner_rows[pair_rows[0]] - owner_rows[pair_rows[1]]  91.1 us
    psum x1, blocking collectives, body(): old_norm = lax.psum(old_part, ('group', 'pencil'))  74.7 us
    psum x1, blocking collectives, body(): norm_next = lax.psum(jnp.sum(resid_next * precond), ('group', 'pencil'))  73.4 us
    unnamed x38, local copies, waits for them, and re-layouts  70.6 us
    scatter x2, local copies, waits for them, and re-layouts, body(): back_rows = jnp.zeros((rows_count,), jnp.float32).at[pair_rows[0]].set(se...  63.2 us
    scatter x1, local copies, waits for them, and re-layouts, load_slab(): jnp.zeros((cycle_total,), jnp.float32).at[positions].set(arrived_rows)  60.8 us
  transfers between devices with their start and end apart: 5, of which 5 were waited for; matrix products, arithmetic and copies ran while one was open for 0% of the time, Pallas kernels for 0%

profile of v1, /device:TPU:1, one launch (start us, length us, event | category | flops | bytes accessed | tf_op | source)
XLA Modules:
  0.0 918.7 jit_solution(9599632266071139603)
XLA Ops:
  9.0 31.2 %scatter_custom_fusion = f32[16384]{0:T(1024)} fusion(s32[8192]{0:T(1024)S(1)} %bitcast.164, f32[8192]{0:T(1024)} %bitcast.154, f32[]{:T(128)} %constant.16.clone.1), kind=kCustom, calls=%fused_computation.81 | custom fusion | bytes 66048 | tf_op jit(solution)/shard_map/scatter | solution.py:131
  40.2 31.9 %scatter_fusion = f32[16384]{0:T(1024)} fusion(f32[16384]{0:T(1024)} %scatter_custom_fusion, s32[8192]{0:T(1024)S(1)} %bitcast.151, f32[8192]{0:T(1024)S(1)} %neg.3), kind=kCustom, calls=%fused_computation.5 | custom fusion | bytes 131072 | tf_op jit(solution)/shard_map/scatter | solution.py:133
  72.1 12.0 %all-to-all-start = ((f32[32,1,512]{2,1,0:T(1,128)}), f32[32,1,512]{2,1,0:T(1,128)S(1)}, u32[]{:S(2)}, u32[]{:S(2)}) async-start(f32[32,1,512]{2,1,0:T(1,128)} %bitcast.11), calls=%async_computation | async-start | bytes 131072 | tf_op jit(solution)/shard_map/all_to_all | solution.py:135
  85.0 8.0 all-to-all-done
  93.0 60.8 %scatter_custom_fusion.2 = f32[24576]{0:T(1024)S(1)} fusion(s32[16384]{0:T(1024)S(1)} %bitcast.160, f32[16384]{0:T(1024)S(1)} %bitcast.167, f32[]{:T(128)} %constant.16.clone.1), kind=kCustom, calls=%fused_computation.72 | custom fusion | bytes 98308 | tf_op jit(solution)/shard_map/scatter | solution.py:62
  154.2 4.0 fusion.8
  158.3 5.2 fusion.16
  163.5 34.5 %copy.165 = f32[8,4,3,64,64]{0,1,2,4,3:T(4,128)} copy(f32[8,4,3,64,64]{3,4,2,0,1:T(8,128)S(1)} %fusion.16) | data formatting | bytes 3145728 | tf_op jit(solution)/shard_map/reshape | solution.py:80
  198.0 31.9 %reshape.388 = f32[8,1,49152]{2,1,0:T(1,128)} reshape(f32[4096,3,4,8]{3,2,1,0:T(4,128)} %bitcast.146) | data formatting | bytes 3145728
  229.8 6.5 all-to-all-start.1
  237.8 19.2 %all-to-all-done.1 = f32[8,1,49152]{2,1,0:T(1,128)S(1)} async-done(((f32[8,1,49152]{2,1,0:T(1,128)}), f32[8,1,49152]{2,1,0:T(1,128)S(1)}, u32[]{:S(2)}, u32[]{:S(2)}) %all-to-all-start.1) | async-done | bytes 1572896 | tf_op jit(solution)/shard_map/all_to_all | solution.py:79
  257.5 4.4 reduce
  261.9 38.7 %reshape.389 = f32[4096,3,4,8]{3,2,1,0:T(4,128)} reshape(f32[8,49152]{1,0:T(8,128)S(1)} %reduce) | data formatting | bytes 3145728
  300.5 20.7 %copy.167 = f32[8,4,3,8,512]{4,0,3,2,1:T(8,128)} copy(f32[8,4,3,8,512]{0,1,2,4,3:T(4,128)} %bitcast.147) | data formatting | bytes 3145728 | tf_op jit(solution)/shard_map/all_to_all | solution.py:79
  321.2 2.6 reshape.305
  323.9 5.1 fusion.5
  329.0 3.2 fusion.2
  334.3 4.6 all-to-all-start.2
  339.6 19.9 %all-to-all-done.2 = f32[64,4,3,512]{3,1,2,0:T(4,128)S(1)} async-done(((f32[64,4,3,512]{3,1,2,0:T(4,128)}), f32[64,4,3,512]{3,1,2,0:T(4,128)S(1)}, u32[]{:S(2)}, u32[]{:S(2)}) %all-to-all-start.2) | async-done | bytes 1572896 | tf_op jit(solution)/shard_map/all_to_all | solution.py:92
  362.1 2.6 reshape.383
  364.7 5.1 fusion.35
  369.9 5.1 fusion.19
  375.0 2.7 fusion.58
  382.4 160.3 %gather_fusion = f32[16384]{0:T(1024)} fusion(f32[24576]{0:T(1024)S(1)} %reshape_reshape.7, s32[16384]{0:T(1024)S(1)} %copy-done.8), kind=kCustom, calls=%fused_computation | custom fusion | bytes 196608 | tf_op jit(solution)/shard_map/gather | solution.py:96
  545.1 96.7 %all-gather.3.cloned.1.call-done = f32[262144]{0:T(1024)} async-done(((f32[1024]{0:T(1024)}), f32[262144]{0:T(1024)}) %all-gather.3.cloned.1.call-update) | async-done | bytes 1048592 | tf_op jit(solution)/shard_map/all_gather | solution.py:144
  643.3 5.6 convolution_bitcast_fusion
  651.4 7.4 all-to-all-start.3
  659.5 8.2 all-to-all-done.3
  667.7 45.5 %gather_fusion.3 = f32[8192]{0:T(1024)S(1)} fusion(f32[16384]{0:T(1024)S(1)} %bitcast.144, s32[8192]{0:T(1024)S(1)} %broadcast_clamp_fusion.1), kind=kCustom, calls=%fused_computation.3 | custom fusion | bytes 98304 | tf_op jit(solution)/shard_map/gather | solution.py:152
  713.2 45.5 %gather_fusion.2 = f32[8192]{0:T(1024)S(1)} fusion(f32[16384]{0:T(1024)S(1)} %bitcast.145, s32[8192]{0:T(1024)S(1)} %broadcast_clamp_fusion.2), kind=kCustom, calls=%fused_computation.2 | custom fusion | bytes 98304 | tf_op jit(solution)/shard_map/gather | solution.py:152
  759.4 74.7 %all-reduce = (f32[]{:T(128)}, f32[]{:T(128)}) all-reduce(f32[]{:T(128)} %fusion.51, f32[]{:T(128)} %get-tuple-element.9), channel_id=1, replica_groups=mesh['group'=32,'pencil'=8] {'group','pencil'}, use_global_device_ids=true, to_apply=%region_1.0 | all-reduce | flops 2 | bytes 16 | tf_op jit(solution)/shard_map/psum | solution.py:127
  836.1 73.4 %psum.23 = f32[]{:T(128)} all-reduce(f32[]{:T(128)} %get-tuple-element.7), channel_id=1, replica_groups=mesh['group'=32,'pencil'=8] {'group','pencil'}, use_global_device_ids=true, to_apply=%region_10.11 | all-reduce | flops 1 | bytes 8 | tf_op jit(solution)/shard_map/psum | solution.py:158
  (87 shorter events, 23.7 us)
Async XLA Ops:
  8.2 64.0 %copy-start.1 = (s32[8192,1]{0,1:T(1,128)}, s32[8192,1]{0,1:T(1,128)S(1)}, u32[]{:S(2)}) copy-start(s32[8192,1]{0,1:T(1,128)S(1)} %get-tuple-element.19) | copy-start | bytes 98308
  8.2 64.0 %copy-start.9 = (s32[8192,1]{0,1:T(1,128)}, s32[8192,1]{0,1:T(1,128)S(1)}, u32[]{:S(2)}) copy-start(s32[8192,1]{0,1:T(1,128)S(1)} %get-tuple-element.20) | copy-start | bytes 98308
  40.2 44.0 %copy-start.11 = (s32[1,1,16384]{2,1,0:T(1,128)S(1)}, s32[1,1,16384]{2,1,0:T(1,128)}, u32[]{:S(2)}) copy-start(s32[1,1,16384]{2,1,0:T(1,128)} %param.20) | copy-start | bytes 196612
  40.2 114.0 %copy-start = (f32[4,3,64,64]{3,2,1,0:T(8,128)S(1)}, f32[4,3,64,64]{3,2,1,0:T(8,128)}, u32[]{:S(2)}) copy-start(f32[4,3,64,64]{3,2,1,0:T(8,128)} %param.16) | copy-start | bytes 589828
  72.1 20.9 %all-to-all-start = ((f32[32,1,512]{2,1,0:T(1,128)}), f32[32,1,512]{2,1,0:T(1,128)S(1)}, u32[]{:S(2)}, u32[]{:S(2)}) async-start(f32[32,1,512]{2,1,0:T(1,128)} %bitcast.11), calls=%async_computation | async-start | bytes 131072 | tf_op jit(solution)/shard_map/all_to_all | solution.py:135
  85.0 8.1 copy-start.6
  229.8 6.5 copy-start.12
  229.8 7.0 copy-start.15
  229.8 27.1 %all-to-all-start.1 = ((f32[8,1,49152]{2,1,0:T(1,128)}), f32[8,1,49152]{2,1,0:T(1,128)S(1)}, u32[]{:S(2)}, u32[]{:S(2)}) async-start(f32[8,1,49152]{2,1,0:T(1,128)} %reshape.388), calls=%async_computation.1 | async-start | bytes 3145728 | tf_op jit(solution)/shard_map/all_to_all | solution.py:79
  323.9 5.1 copy-start.13
  332.2 6.7 copy-start.16
  334.3 4.6 copy-start.7
  334.3 25.2 %all-to-all-start.2 = ((f32[64,4,3,512]{3,1,2,0:T(4,128)}), f32[64,4,3,512]{3,1,2,0:T(4,128)S(1)}, u32[]{:S(2)}, u32[]{:S(2)}) async-start(f32[64,4,3,512]{3,1,2,0:T(4,128)} %copy.149), calls=%async_computation.2 | async-start | bytes 3145728 | tf_op jit(solution)/shard_map/all_to_all | solution.py:92
  338.9 302.9 %all-gather.3.cloned.1.call-start = ((), (), s32[]{:S(2)}) async-start(), calls=%async_computation.4 | async-start | bytes 1052672 | tf_op jit(solution)/shard_map/all_gather | solution.py:144
  377.8 4.6 copy-start.8
  382.4 161.9 %copy-start.17 = (s32[1,1,32]{2,1,0:T(1,128)S(1)}, s32[1,1,32]{2,1,0:T(1,128)}, u32[]{:S(2)}) copy-start(s32[1,1,32]{2,1,0:T(1,128)} %param.23) | copy-start | bytes 388
  382.4 162.7 %copy-start.2 = (s32[8192,1]{0,1:T(1,128)S(1)}, s32[8192,1]{0,1:T(1,128)}, u32[]{:S(2)}) copy-start(s32[8192,1]{0,1:T(1,128)} %copy-done.1) | copy-start | bytes 98308
  643.2 15.6 %copy-start.10 = (s32[8192,1]{0,1:T(1,128)S(1)}, s32[8192,1]{0,1:T(1,128)}, u32[]{:S(2)}) copy-start(s32[8192,1]{0,1:T(1,128)} %copy-done.9) | copy-start | bytes 98308
  643.2 15.6 %copy-start.4 = (f32[1,1,8192]{2,1,0:T(1,128)S(1)}, f32[1,1,8192]{2,1,0:T(1,128)}, u32[]{:S(2)}) copy-start(f32[1,1,8192]{2,1,0:T(1,128)} %param.15) | copy-start | bytes 98308
  643.2 15.6 %copy-start.5 = (f32[1,1,8192]{2,1,0:T(1,128)S(1)}, f32[1,1,8192]{2,1,0:T(1,128)}, u32[]{:S(2)}) copy-start(f32[1,1,8192]{2,1,0:T(1,128)} %param.13) | copy-start | bytes 98308
  651.4 16.3 %all-to-all-start.3 = ((f32[32,1,512]{2,1,0:T(1,128)}), f32[32,1,512]{2,1,0:T(1,128)S(1)}, u32[]{:S(2)}, u32[]{:S(2)}) async-start(f32[32,1,512]{2,1,0:T(1,128)} %bitcast.57), calls=%async_computation.3 | async-start | bytes 131072 | tf_op jit(solution)/shard_map/all_to_all | solution.py:149
  713.2 45.6 %copy-start.3 = (f32[1,1,8192]{2,1,0:T(1,128)S(1)}, f32[1,1,8192]{2,1,0:T(1,128)}, u32[]{:S(2)}) copy-start(f32[1,1,8192]{2,1,0:T(1,128)} %param.14) | copy-start | bytes 98308
  713.2 197.6 %copy-start.14 = (f32[1,1,8192]{2,1,0:T(1,128)S(1)}, f32[1,1,8192]{2,1,0:T(1,128)}, u32[]{:S(2)}) copy-start(f32[1,1,8192]{2,1,0:T(1,128)} %param.12) | copy-start | bytes 98308
Sparse Core Ops, SparseCore 0:
  545.2 96.5 all-gather.2
